TPU v7x, 128 devices: a whole 4x4x4 slice. The times are simulated.
128 devices in a mesh: outer: 2 (over y_hi), inner: 64 (over z, x, y_lo, core).
Axes of the slice: x: 4, y: 4 (y_hi: 2, y_lo: 2; y = y_hi * 2 + y_lo), z: 4, core: 2. Of those that a mesh axis runs over, the one named last changes fastest.
Arguments:
- tile_counts: int32 [128, 4, 1024, 512], P(('outer', 'inner')), may hold values from 0 to 63, as said below
- row_counts: int32 [131072], P(('outer', 'inner')), may hold values from 100 to 19999
- col_counts: int32 [65536], P(('outer', 'inner')), may hold values from 100 to 19999
- row_factors: float32 [131072, 256], P(('outer', 'inner')), may hold values from -1.8 to 1.8
- row_accum: float32 [131072, 256], P(('outer', 'inner')), may hold values from 1 to 10
- col_factors: float32 [65536, 256], P(('outer', 'inner')), may hold values from -1.8 to 1.8
- col_accum: float32 [65536, 256], P(('outer', 'inner')), may hold values from 1 to 10
Outputs:
- rows_final: float32 [131072, 256], P(('outer', 'inner'))
- row_accum_final: float32 [131072, 256], P(('outer', 'inner'))
- cols_final: float32 [65536, 256], P(('outer', 'inner'))
- col_accum_final: float32 [65536, 256], P(('outer', 'inner'))
Inputs may be any that keep to these rules, and one draw needn't show every extreme that they name: `tile_counts`: Co-occurrence counts; about half of them are zero.
All inputs are finite; a program needn't handle non-finite values.
Results may differ from a plain program's by a relative error of at most 0.0003.
Values sent between devices are 32-bit elements; how exact they have to be, the bound alone decides.
No kernel may reach another device: no remote copies, remote signals or barrier semaphores. Data moves between devices by JAX's collectives and lax.ppermute only.
A program may use at most 64 MiB of HBM per device.

v0:
```python
import functools

import jax
import jax.numpy as jnp
from jax import lax
from jax.experimental import pallas as pl
from jax.experimental.pallas import tpu as pltpu
from jax.sharding import PartitionSpec as P


LOG_TOTAL = 17.0
LEARNING = 0.05
HALVES = 2
f32 = jnp.float32
V, H, DMA = pltpu.VMEM, pltpu.HBM, pltpu.SemaphoreType.DMA


def dot(a, b, ca, cb):
    return lax.dot_general(
        a, b, (((ca,), (cb,)), ((), ())), precision=lax.Precision.HIGH, preferred_element_type=f32
    )


def adagrad(value, total, grad):
    total = total + grad * grad
    return value - LEARNING * (grad * lax.rsqrt(total)), total


def fetches(pairs, sems):
    copies = [pltpu.make_async_copy(src, dst, sems.at[i]) for i, (src, dst) in enumerate(pairs)]
    for copy in copies:
        copy.start()
    return copies


def row_spans(n, size):
    return [pl.ds(start, size) for start in range(0, n, size)]


def put_terms(x, row_logs, first, t_ref, c_ref, rows):
    m = jnp.maximum(x.astype(f32), 1.0)
    lanes = row_logs.shape[0]
    logs = [row_logs[:, j : j + 1] for j in range(first, first + x.shape[0] // lanes)]
    t_ref[rows, :] = jnp.log(m) - jnp.concatenate(logs, axis=0)
    c_ref[rows, :] = jnp.where(x > 0, 0.1 + 0.25 * (m * lax.rsqrt(m)), 0.0)


def errors(z, target, confidence, col_logs):
    gap = (z - target) + col_logs
    return jnp.where(confidence > 0.0, confidence * gap, 0.5 * jnp.tanh(0.5 * gap) + 0.5)


def shifted_row_logs(rows_ref):
    return jnp.log(rows_ref[...].astype(f32)).T - LOG_TOTAL


def terms_kernel(step, x_hbm, rows_ref, t_ref, c_ref, x_buf, sems):
    spans = row_spans(x_buf.shape[0], 256)
    copies = fetches([(x_hbm.at[0, step, rows], x_buf.at[rows]) for rows in spans], sems)
    row_logs = shifted_row_logs(rows_ref)
    for i, rows in enumerate(spans):
        copies[i].wait()
        put_terms(x_buf[rows, :], row_logs, 2 * i, t_ref, c_ref, rows)


def first_kernel(
    x_hbm, rows_hbm, cols_hbm, W_hbm, A_hbm, C_hbm, B_hbm, Wo_ref, Ao_ref, t_ref, c_ref, h_ref, *rest
):
    M_refs, B_refs = rest[:HALVES], rest[HALVES : 2 * HALVES]
    x_buf, W_buf, A_buf, rows_buf, cols_buf, sems, late_sems = rest[2 * HALVES :]
    n, width = B_refs[0].shape
    quarters, spans = row_spans(x_buf.shape[0], 256), row_spans(x_buf.shape[0], 512)
    pairs = [(cols_hbm, cols_buf), (rows_hbm, rows_buf)]
    pairs += [(C_hbm.at[pl.ds(j * n, n)], M_refs[j].at[pl.ds(0, n)]) for j in range(HALVES)]
    head = len(pairs)
    pairs += [(x_hbm.at[0, 0, rows], x_buf.at[rows]) for rows in quarters]
    body = len(pairs)
    for rows in spans:
        pairs.append((W_hbm.at[rows], W_buf.at[rows]))
        pairs.append((A_hbm.at[rows], A_buf.at[rows]))
    copies = fetches(pairs, sems)
    late = fetches([(B_hbm.at[pl.ds(j * n, n)], B_refs[j]) for j in range(HALVES)], late_sems)
    for copy in copies[:2]:
        copy.wait()
    col_logs = jnp.log(cols_buf[...].astype(f32))
    row_logs = shifted_row_logs(rows_buf)
    for i, rows in enumerate(quarters):
        copies[head + i].wait()
        put_terms(x_buf[rows, :], row_logs, 2 * i, t_ref, c_ref, rows)
    for copy in copies[2:head]:
        copy.wait()
    for j in range(HALVES):
        M_refs[j][n:, :] = jnp.broadcast_to(col_logs[:, j * n : (j + 1) * n], (8, width))
    C = jnp.concatenate([ref[:n, :] for ref in M_refs], axis=0)
    for i, rows in enumerate(spans):
        for copy in copies[body + 2 * i : body + 2 * i + 2]:
            copy.wait()
        W = W_buf[rows, :]
        e = errors(dot(W, C, 1, 1), t_ref[rows, :], c_ref[rows, :], col_logs)
        Wo_ref[rows, :], Ao_ref[rows, :] = adagrad(W, A_buf[rows, :], dot(e, C, 1, 0))
    h_ref[...] = col_gradient((0,), t_ref, c_ref, M_refs[:1], Wo_ref)
    for copy in late:
        copy.wait()


def col_gradient(halves, t_ref, c_ref, M_refs, W_ref):
    n = M_refs[0].shape[1]
    cols = pl.ds(halves[0] * n, len(halves) * n)
    C = jnp.concatenate([ref[:n, :] for ref in M_refs], axis=0)
    col_logs = jnp.concatenate([ref[n : n + 1, :] for ref in M_refs], axis=1)
    grad = None
    for rows in row_spans(W_ref.shape[0], 256):
        W = W_ref[rows, :]
        part = dot(errors(dot(W, C, 1, 1), t_ref[rows, cols], c_ref[rows, cols], col_logs), W, 0, 0)
        grad = part if grad is None else grad + part
    return grad


def half_errors(j, W, t_ref, c_ref, M_ref, rows):
    n = M_ref.shape[1]
    cols = pl.ds(j * n, n)
    C = M_ref[:n, :]
    e = errors(dot(W, C, 1, 1), t_ref[rows, cols], c_ref[rows, cols], M_ref[n : n + 1, :])
    return e, C


def row_part_kernel(t_ref, c_ref, M_ref, W_ref, g_ref):
    for rows in row_spans(W_ref.shape[0], 256):
        e, C = half_errors(0, W_ref[rows, :], t_ref, c_ref, M_ref, rows)
        g_ref[rows, :] = dot(e, C, 1, 0)


def row_col_kernel(
    size, halves, after, t_ref, c_ref, M0_ref, M1_ref, W_ref, A_ref, g_ref, Wo_ref, Ao_ref, *h_refs
):
    for rows in row_spans(W_ref.shape[0], size):
        W = W_ref[rows, :]
        e, C = half_errors(1, W, t_ref, c_ref, M1_ref, rows)
        Wo_ref[rows, :], Ao_ref[rows, :] = adagrad(W, A_ref[rows, :], g_ref[rows, :] + dot(e, C, 1, 0))
        after(rows)
    grad = col_gradient(halves, t_ref, c_ref, (M0_ref, M1_ref)[: len(halves)], Wo_ref)
    for j, h_ref in enumerate(h_refs):
        n = h_ref.shape[0]
        h_ref[...] = grad[j * n : (j + 1) * n, :]


def last_kernel(*refs):
    ins, (Wo_hbm, Ao_hbm, h0_ref, h1_ref, W_buf, A_buf, sems) = refs[:7], refs[7:]
    stores = []

    def after(rows):
        pairs = [(W_buf.at[rows], Wo_hbm.at[rows]), (A_buf.at[rows], Ao_hbm.at[rows])]
        stores.extend(fetches(pairs, sems.at[len(stores) // 2]))

    row_col_kernel(512, (0, 1), after, *ins, W_buf, A_buf, h0_ref, h1_ref)
    for copy in stores:
        copy.wait()


def col_kernel(j, t_ref, c_ref, M_ref, W_ref, h_ref):
    h_ref[...] = col_gradient((j,), t_ref, c_ref, (M_ref,), W_ref)


def update_kernel(h_ref, M_ref, B_ref, Mo_ref, Bo_ref):
    n = h_ref.shape[0]
    Mo_ref[:n, :], Bo_ref[...] = adagrad(M_ref[:n, :], B_ref[...], h_ref[...])
    Mo_ref[n:, :] = M_ref[n:, :]


def final_kernel(*refs):
    ins, (Co_ref, Bo_ref) = refs[:-2], refs[-2:]
    n = ins[0].shape[0]
    for j in range(HALVES):
        h_ref, M_ref, B_ref = ins[3 * j : 3 * j + 3]
        rows = pl.ds(j * n, n)
        Co_ref[rows, :], Bo_ref[rows, :] = adagrad(M_ref[:n, :], B_ref[...], h_ref[...])


def call(kernel, operands, spaces, outs, out_spaces, scratch, mib):
    return pl.pallas_call(
        kernel,
        in_specs=[pl.BlockSpec(memory_space=s) for s in spaces],
        out_specs=[pl.BlockSpec(memory_space=s) for s in out_spaces],
        out_shape=[jax.ShapeDtypeStruct(s, f32) for s in outs],
        scratch_shapes=scratch,
        compiler_params=pltpu.CompilerParams(vmem_limit_bytes=mib << 20),
    )(*operands)


def body(tile_counts, row_counts, col_counts, row_factors, row_accum, col_factors, col_accum):
    steps = tile_counts.shape[1]
    n_outer, n_inner = lax.axis_size("outer"), lax.axis_size("inner")

    def move(block, across):
        route = [
            (o * n_inner + i, (o + across) % n_outer * n_inner + (i + 1) % n_inner)
            for o in range(n_outer)
            for i in range(n_inner)
        ]
        return lax.ppermute(block, ("outer", "inner"), route)

    rows = row_counts.reshape(-1, 128)
    cols = col_counts.reshape(1, -1)
    hbm = [tile_counts, rows, cols, row_factors, row_accum, col_factors, col_accum]
    hbm = [pltpu.with_memory_space_constraint(a, H) for a in hbm]
    wide, tall = row_factors.shape, col_factors.shape
    tile = tile_counts.shape[2:]
    half = (tall[0] // HALVES, tall[1])
    message = (half[0] + 8, half[1])
    W, A, t, c, first_grad, *blocks = call(
        first_kernel, hbm, [H] * 7,
        [wide, wide, tile, tile, half] + [message] * HALVES + [half] * HALVES, [V] * (5 + 2 * HALVES),
        [V(tile, jnp.int32), V(wide, f32), V(wide, f32), V(rows.shape, jnp.int32),
         V(cols.shape, jnp.int32), DMA((2 + HALVES + 4 + 2 * 2,)), DMA((HALVES,))],
        24,
    )
    M, B = blocks[:HALVES], blocks[HALVES:]
    for step in range(steps):
        grads = [first_grad]
        if step > 0:
            g = call(row_part_kernel, (t, c, M[0], W), [V] * 4, [wide], [V], [], 12)[0]
            operands = (t, c, M[0], M[1], W, A, g)
            if step + 1 == steps:
                W, A, *grads = call(
                    last_kernel, operands, [V] * 7, [wide, wide, half, half], [H, H, V, V],
                    [V(wide, f32), V(wide, f32), DMA((2, 2))], 20,
                )
                break
            size, halves = 512, tuple(range(HALVES))
            W, A, *grads = call(
                functools.partial(row_col_kernel, size, halves, lambda rows: None), operands, [V] * 7,
                [wide, wide] + [half] * len(halves), [V] * (2 + len(halves)), [], 20,
            )
        across = int(step + 1 == steps // 2)
        sent, sums = [], []
        for j in range(HALVES):
            if j == len(grads):
                operands = (t, c, M[j], W)
                grads += call(functools.partial(col_kernel, j), operands, [V] * 4, [half], [V], [], 12)
            value, total = call(update_kernel, (grads[j], M[j], B[j]), [V] * 3, [message, half], [V] * 2, [], 4)
            sent.append(move(value, across))
            sums.append(total)
        row_tie = lax.optimization_barrier((rows, *sums))[0]
        t, c = call(
            functools.partial(terms_kernel, step + 1), (hbm[0], row_tie), [H, V], [tile, tile], [V] * 2,
            [V(tile, jnp.int32), DMA((4,))], 12,
        )
        M, B = sent, [move(total, across) for total in sums]
    operands = (grads[0], M[0], B[0], grads[1], M[1], B[1])
    C, B = call(final_kernel, operands, [V] * 6, [tall, tall], [V] * 2, [], 6)
    return W, A, C, B


def solution(mesh):
    both = ("outer", "inner")
    return jax.shard_map(
        body,
        mesh=mesh,
        in_specs=(P(both, None, None, None), P(both), P(both)) + (P(both, None),) * 4,
        out_specs=(P(both, None),) * 4,
        check_vma=False,
    )
```

profile of v0, /device:TPU:0, one launch (start us, length us, event | category | flops | bytes accessed | tf_op | source)
XLA Modules:
  0.0 69.5 jit_solution(13506889391682252979)
XLA Ops:
  0.6 6.4 %shard_map.102 = (f32[1024,256]{1,0:T(8,128)S(1)}, f32[1024,256]{1,0:T(8,128)S(1)}, f32[1024,512]{1,0:T(8,128)S(1)}, f32[1024,512]{1,0:T(8,128)S(1)}, f32[256,25...) custom-call(s32[1,4,1024,512]{3,2,1,0:T(8,128)} %x_hbm.7, ...), custom_call_target="tpu_custom_call" | custom-call | tf_op jit(solution)/shard_map/pallas_call | solution.py:180
  7.2 1.6 %shard_map.104.h_ref = f32[256,256]{1,0:T(8,128)S(1)} custom-call(f32[1024,512]{1,0:T(8,128)S(1)} %get-tuple-element.52.t_ref, f32[1024,512]{1,0:T(8,128)S(1)} %get-tuple-element.53.c_ref, f32[264,256]{1,0:T(8,128)S(1)} %get-tuple-element.54.M_ref, f32[1024,256]{1,0:T(8,128)S(1)} %get-tuple-element.55.W_ref), custom_call_target="tpu_custom_call" | custom-call | tf_op jit(solution)/shard_map/pallas_call | solution.py:180
  8.9 1.8 %collective-permute-start.1 = (f32[264,256]{1,0:T(8,128)S(1)}, f32[264,256]{1,0:T(8,128)S(1)}, u32[]{:S(2)}, u32[]{:S(2)}) collective-permute-start(f32[264,256]{1,0:T(8,128)S(1)} %get-tuple-element.62), channel_id=1, source_target_pairs={{0,1},{1,2},{2,3},{3,4},{4,5},{5,6},{6,7},{7,8},{8,9},{9,10},{10,1... | collective-permute-start | bytes 811016 | tf_op jit(solution)/shard_map/ppermute | solution.py:200
  10.8 1.4 %collective-permute-start.3 = (f32[256,256]{1,0:T(8,128)S(1)}, f32[256,256]{1,0:T(8,128)S(1)}, u32[]{:S(2)}, u32[]{:S(2)}) collective-permute-start(f32[256,256]{1,0:T(8,128)S(1)} %get-tuple-element.57), channel_id=1, source_target_pairs={{0,1},{1,2},{2,3},{3,4},{4,5},{5,6},{6,7},{7,8},{8,9},{9,10},{10,1... | collective-permute-start | bytes 786440 | tf_op jit(solution)/shard_map/ppermute | solution.py:200
  12.3 1.9 %shard_map.106 = (f32[1024,512]{1,0:T(8,128)S(1)}, f32[1024,512]{1,0:T(8,128)S(1)}) custom-call(s32[1,4,1024,512]{3,2,1,0:T(8,128)} %x_hbm.7, s32[8,128]{1,0:T(8,128)S(1)} %bitcast.3), custom_call_target="tpu_custom_call" | custom-call | tf_op jit(solution)/shard_map/pallas_call | solution.py:180
  14.2 4.0 %collective-permute-done.M_ref.M0_ref = f32[264,256]{1,0:T(8,128)S(1)} collective-permute-done((f32[264,256]{1,0:T(8,128)S(1)}, f32[264,256]{1,0:T(8,128)S(1)}, u32[]{:S(2)}, u32[]{:S(2)}) %collective-permute-start) | collective-permute-done | bytes 270368 | tf_op jit(solution)/shard_map/ppermute | solution.py:200
  18.1 1.6 %shard_map.107.g_ref = f32[1024,256]{1,0:T(8,128)S(1)} custom-call(f32[1024,512]{1,0:T(8,128)S(1)} %get-tuple-element.59.t_ref, f32[1024,512]{1,0:T(8,128)S(1)} %get-tuple-element.60.c_ref, f32[264,256]{1,0:T(8,128)S(1)} %collective-permute-done.M_ref.M0_ref, f32[1024,256]{1,0:T(8,128)S(1)} %get-tuple-element.55.W_ref), custom_call_target="tpu_custom_call" | custom-call | tf_op jit(solution)/shard_map/pallas_call | solution.py:180
  19.7 1.3 %collective-permute-done.1.M1_ref.M_ref = f32[264,256]{1,0:T(8,128)S(1)} collective-permute-done((f32[264,256]{1,0:T(8,128)S(1)}, f32[264,256]{1,0:T(8,128)S(1)}, u32[]{:S(2)}, u32[]{:S(2)}) %collective-permute-start.1) | collective-permute-done | bytes 270368 | tf_op jit(solution)/shard_map/ppermute | solution.py:200
  21.0 3.8 %shard_map.108 = (f32[1024,256]{1,0:T(8,128)S(1)}, f32[1024,256]{1,0:T(8,128)S(1)}, f32[256,256]{1,0:T(8,128)S(1)}, f32[256,256]{1,0:T(8,128)S(1)}) custom-call(f32[1024,512]{1,0:T(8,128)S(1)} %get-tuple-element.59.t_ref, f32[1024,512]{1,0:T(8,128)S(1)} %get-tuple-element.60.c_ref, f32[264,256]{1,0:T(8,128)S(1)} %collective-permute-done.M_ref.M0_ref, ...), custom_call_target="tpu_custom_call" | custom-call | tf_op jit(solution)/shard_map/pallas_call | solution.py:180
  25.0 1.7 %collective-permute-done.3.B_ref = f32[256,256]{1,0:T(8,128)S(1)} collective-permute-done((f32[256,256]{1,0:T(8,128)S(1)}, f32[256,256]{1,0:T(8,128)S(1)}, u32[]{:S(2)}, u32[]{:S(2)}) %collective-permute-start.3) | collective-permute-done | bytes 262176 | tf_op jit(solution)/shard_map/ppermute | solution.py:200
  27.6 1.9 %shard_map.111 = (f32[1024,512]{1,0:T(8,128)S(1)}, f32[1024,512]{1,0:T(8,128)S(1)}) custom-call(s32[1,4,1024,512]{3,2,1,0:T(8,128)} %x_hbm.7, s32[8,128]{1,0:T(8,128)S(1)} %bitcast.4), custom_call_target="tpu_custom_call" | custom-call | tf_op jit(solution)/shard_map/pallas_call | solution.py:180
  29.5 9.0 %collective-permute-done.4.M_ref.M0_ref = f32[264,256]{1,0:T(8,128)S(1)} collective-permute-done((f32[264,256]{1,0:T(8,128)S(1)}, f32[264,256]{1,0:T(8,128)S(1)}, u32[]{:S(2)}, u32[]{:S(2)}) %collective-permute-start.4) | collective-permute-done | bytes 270368 | tf_op jit(solution)/shard_map/ppermute | solution.py:200
  38.5 1.6 %shard_map.112.g_ref = f32[1024,256]{1,0:T(8,128)S(1)} custom-call(f32[1024,512]{1,0:T(8,128)S(1)} %get-tuple-element.69.t_ref, f32[1024,512]{1,0:T(8,128)S(1)} %get-tuple-element.70.c_ref, f32[264,256]{1,0:T(8,128)S(1)} %collective-permute-done.4.M_ref.M0_ref, f32[1024,256]{1,0:T(8,128)S(1)} %get-tuple-element.73.W_ref), custom_call_target="tpu_custom_call" | custom-call | tf_op jit(solution)/shard_map/pallas_call | solution.py:180
  40.1 3.2 %collective-permute-done.5.M1_ref.M_ref = f32[264,256]{1,0:T(8,128)S(1)} collective-permute-done((f32[264,256]{1,0:T(8,128)S(1)}, f32[264,256]{1,0:T(8,128)S(1)}, u32[]{:S(2)}, u32[]{:S(2)}) %collective-permute-start.5) | collective-permute-done | bytes 270368 | tf_op jit(solution)/shard_map/ppermute | solution.py:200
  43.2 3.7 %shard_map.113 = (f32[1024,256]{1,0:T(8,128)S(1)}, f32[1024,256]{1,0:T(8,128)S(1)}, f32[256,256]{1,0:T(8,128)S(1)}, f32[256,256]{1,0:T(8,128)S(1)}) custom-call(f32[1024,512]{1,0:T(8,128)S(1)} %get-tuple-element.69.t_ref, f32[1024,512]{1,0:T(8,128)S(1)} %get-tuple-element.70.c_ref, f32[264,256]{1,0:T(8,128)S(1)} %collective-permute-done.4.M_ref.M0_ref, ...), custom_call_target="tpu_custom_call" | custom-call | tf_op jit(solution)/shard_map/pallas_call | solution.py:180
  47.0 0.9 %collective-permute-done.6.B_ref = f32[256,256]{1,0:T(8,128)S(1)} collective-permute-done((f32[256,256]{1,0:T(8,128)S(1)}, f32[256,256]{1,0:T(8,128)S(1)}, u32[]{:S(2)}, u32[]{:S(2)}) %collective-permute-start.6) | collective-permute-done | bytes 262176 | tf_op jit(solution)/shard_map/ppermute | solution.py:200
  48.7 3.9 %collective-permute-done.7.B_ref = f32[256,256]{1,0:T(8,128)S(1)} collective-permute-done((f32[256,256]{1,0:T(8,128)S(1)}, f32[256,256]{1,0:T(8,128)S(1)}, u32[]{:S(2)}, u32[]{:S(2)}) %collective-permute-start.7) | collective-permute-done | bytes 262176 | tf_op jit(solution)/shard_map/ppermute | solution.py:200
  53.9 1.9 %shard_map.116 = (f32[1024,512]{1,0:T(8,128)S(1)}, f32[1024,512]{1,0:T(8,128)S(1)}) custom-call(s32[1,4,1024,512]{3,2,1,0:T(8,128)} %x_hbm.7, s32[8,128]{1,0:T(8,128)S(1)} %bitcast.5), custom_call_target="tpu_custom_call" | custom-call | tf_op jit(solution)/shard_map/pallas_call | solution.py:180
  55.8 2.3 %collective-permute-done.8.M_ref.refs_2_.refs_1_ = f32[264,256]{1,0:T(8,128)S(1)} collective-permute-done((f32[264,256]{1,0:T(8,128)S(1)}, f32[264,256]{1,0:T(8,128)S(1)}, u32[]{:S(2)}, u32[]{:S(2)}) %collective-permute-start.8) | collective-permute-done | bytes 270368 | tf_op jit(solution)/shard_map/ppermute | solution.py:200
  58.2 1.6 %shard_map.117.refs_6_ = f32[1024,256]{1,0:T(8,128)S(1)} custom-call(f32[1024,512]{1,0:T(8,128)S(1)} %get-tuple-element.80.t_ref.refs_0_, f32[1024,512]{1,0:T(8,128)S(1)} %get-tuple-element.81.c_ref.refs_1_, f32[264,256]{1,0:T(8,128)S(1)} %collective-permute-done.8.M_ref.refs_2_.refs_1_, f32[1024,256]{1,0:T(8,128)S(1)} %get-tuple-element.84.W_ref.refs_4_), custom_call_target="tpu_custom_call" | custom-call | tf_op jit(solution)/shard_map/pallas_call | solution.py:180
  59.7 3.1 %collective-permute-done.9.refs_3_.refs_4_ = f32[264,256]{1,0:T(8,128)S(1)} collective-permute-done((f32[264,256]{1,0:T(8,128)S(1)}, f32[264,256]{1,0:T(8,128)S(1)}, u32[]{:S(2)}, u32[]{:S(2)}) %collective-permute-start.9) | collective-permute-done | bytes 270368 | tf_op jit(solution)/shard_map/ppermute | solution.py:200
  62.8 4.0 %shard_map.118 = (f32[1024,256]{1,0:T(8,128)}, f32[1024,256]{1,0:T(8,128)}, f32[256,256]{1,0:T(8,128)S(1)}, f32[256,256]{1,0:T(8,128)S(1)}) custom-call(f32[1024,512]{1,0:T(8,128)S(1)} %get-tuple-element.80.t_ref.refs_0_, f32[1024,512]{1,0:T(8,128)S(1)} %get-tuple-element.81.c_ref.refs_1_, f32[264,256]{1,0:T(8,128)S(1)} %collective-permute-done.8.M_ref.refs_2_.refs_1_, ...), custom_call_target="tpu_custom_call" | custom-call | tf_op jit(solution)/shard_map/pallas_call | solution.py:180
  66.9 1.6 %collective-permute-done.10.refs_2_ = f32[256,256]{1,0:T(8,128)S(1)} collective-permute-done((f32[256,256]{1,0:T(8,128)S(1)}, f32[256,256]{1,0:T(8,128)S(1)}, u32[]{:S(2)}, u32[]{:S(2)}) %collective-permute-start.10) | collective-permute-done | bytes 262176 | tf_op jit(solution)/shard_map/ppermute | solution.py:200
  68.4 1.1 %shard_map.119 = (f32[512,256]{1,0:T(8,128)}, f32[512,256]{1,0:T(8,128)}) custom-call(f32[256,256]{1,0:T(8,128)S(1)} %get-tuple-element.88.refs_0_, f32[264,256]{1,0:T(8,128)S(1)} %collective-permute-done.8.M_ref.refs_2_.refs_1_, f32[256,256]{1,0:T(8,128)S(1)} %collective-permute-done.10.refs_2_, f32[256,256]{1,0:T(8,128)S(1)} %get-tuple-element.89.refs_3_, ...), custom_call_target="tpu_custom_call" | custom-call | tf_op jit(solution)/shard_map/pallas_call | solution.py:180
  (20 shorter events, 3.5 us)
Async XLA Ops:
  7.1 11.0 %collective-permute-start = (f32[264,256]{1,0:T(8,128)S(1)}, f32[264,256]{1,0:T(8,128)S(1)}, u32[]{:S(2)}, u32[]{:S(2)}) collective-permute-start(f32[264,256]{1,0:T(8,128)S(1)} %get-tuple-element.61), channel_id=1, source_target_pairs={{0,1},{1,2},{2,3},{3,4},{4,5},{5,6},{6,7},{7,8},{8,9},{9,10},{10,1... | collective-permute-start | bytes 811016 | tf_op jit(solution)/shard_map/ppermute | solution.py:200
  7.2 5.1 %copy-start = (s32[1024]{0:T(1024)S(1)}, s32[1024]{0:T(1024)}, u32[]{:S(2)}) copy-start(s32[1024]{0:T(1024)} %param.8) | copy-start | bytes 12292
  8.9 12.1 %collective-permute-start.1 = (f32[264,256]{1,0:T(8,128)S(1)}, f32[264,256]{1,0:T(8,128)S(1)}, u32[]{:S(2)}, u32[]{:S(2)}) collective-permute-start(f32[264,256]{1,0:T(8,128)S(1)} %get-tuple-element.62), channel_id=1, source_target_pairs={{0,1},{1,2},{2,3},{3,4},{4,5},{5,6},{6,7},{7,8},{8,9},{9,10},{10,1... | collective-permute-start | bytes 811016 | tf_op jit(solution)/shard_map/ppermute | solution.py:200
  10.8 14.1 %collective-permute-start.2 = (f32[256,256]{1,0:T(8,128)S(1)}, f32[256,256]{1,0:T(8,128)S(1)}, u32[]{:S(2)}, u32[]{:S(2)}) collective-permute-start(f32[256,256]{1,0:T(8,128)S(1)} %get-tuple-element.51), channel_id=1, source_target_pairs={{0,1},{1,2},{2,3},{3,4},{4,5},{5,6},{6,7},{7,8},{8,9},{9,10},{10,1... | collective-permute-start | bytes 786440 | tf_op jit(solution)/shard_map/ppermute | solution.py:200
  10.8 15.8 %collective-permute-start.3 = (f32[256,256]{1,0:T(8,128)S(1)}, f32[256,256]{1,0:T(8,128)S(1)}, u32[]{:S(2)}, u32[]{:S(2)}) collective-permute-start(f32[256,256]{1,0:T(8,128)S(1)} %get-tuple-element.57), channel_id=1, source_target_pairs={{0,1},{1,2},{2,3},{3,4},{4,5},{5,6},{6,7},{7,8},{8,9},{9,10},{10,1... | collective-permute-start | bytes 786440 | tf_op jit(solution)/shard_map/ppermute | solution.py:200
  24.9 13.6 %collective-permute-start.4 = (f32[264,256]{1,0:T(8,128)S(1)}, f32[264,256]{1,0:T(8,128)S(1)}, u32[]{:S(2)}, u32[]{:S(2)}) collective-permute-start(f32[264,256]{1,0:T(8,128)S(1)} %get-tuple-element.71), channel_id=1, source_target_pairs={{0,65},{1,66},{2,67},{3,68},{4,69},{5,70},{6,71},{7,72},{8,73},{9,... | collective-permute-start | bytes 811016 | tf_op jit(solution)/shard_map/ppermute | solution.py:200
  26.7 16.5 %collective-permute-start.5 = (f32[264,256]{1,0:T(8,128)S(1)}, f32[264,256]{1,0:T(8,128)S(1)}, u32[]{:S(2)}, u32[]{:S(2)}) collective-permute-start(f32[264,256]{1,0:T(8,128)S(1)} %get-tuple-element.72), channel_id=1, source_target_pairs={{0,65},{1,66},{2,67},{3,68},{4,69},{5,70},{6,71},{7,72},{8,73},{9,... | collective-permute-start | bytes 811016 | tf_op jit(solution)/shard_map/ppermute | solution.py:200
  26.8 21.1 %collective-permute-start.6 = (f32[256,256]{1,0:T(8,128)S(1)}, f32[256,256]{1,0:T(8,128)S(1)}, u32[]{:S(2)}, u32[]{:S(2)}) collective-permute-start(f32[256,256]{1,0:T(8,128)S(1)} %get-tuple-element.65), channel_id=1, source_target_pairs={{0,65},{1,66},{2,67},{3,68},{4,69},{5,70},{6,71},{7,72},{8,73},{9,... | collective-permute-start | bytes 786440 | tf_op jit(solution)/shard_map/ppermute | solution.py:200
  26.9 25.7 %collective-permute-start.7 = (f32[256,256]{1,0:T(8,128)S(1)}, f32[256,256]{1,0:T(8,128)S(1)}, u32[]{:S(2)}, u32[]{:S(2)}) collective-permute-start(f32[256,256]{1,0:T(8,128)S(1)} %get-tuple-element.67), channel_id=1, source_target_pairs={{0,65},{1,66},{2,67},{3,68},{4,69},{5,70},{6,71},{7,72},{8,73},{9,... | collective-permute-start | bytes 786440 | tf_op jit(solution)/shard_map/ppermute | solution.py:200
  48.0 10.2 %collective-permute-start.8 = (f32[264,256]{1,0:T(8,128)S(1)}, f32[264,256]{1,0:T(8,128)S(1)}, u32[]{:S(2)}, u32[]{:S(2)}) collective-permute-start(f32[264,256]{1,0:T(8,128)S(1)} %get-tuple-element.82), channel_id=1, source_target_pairs={{0,1},{1,2},{2,3},{3,4},{4,5},{5,6},{6,7},{7,8},{8,9},{9,10},{10,1... | collective-permute-start | bytes 811016 | tf_op jit(solution)/shard_map/ppermute | solution.py:200
  52.7 10.2 %collective-permute-start.9 = (f32[264,256]{1,0:T(8,128)S(1)}, f32[264,256]{1,0:T(8,128)S(1)}, u32[]{:S(2)}, u32[]{:S(2)}) collective-permute-start(f32[264,256]{1,0:T(8,128)S(1)} %get-tuple-element.83), channel_id=1, source_target_pairs={{0,1},{1,2},{2,3},{3,4},{4,5},{5,6},{6,7},{7,8},{8,9},{9,10},{10,1... | collective-permute-start | bytes 811016 | tf_op jit(solution)/shard_map/ppermute | solution.py:200
  53.5 13.4 %collective-permute-start.11 = (f32[256,256]{1,0:T(8,128)S(1)}, f32[256,256]{1,0:T(8,128)S(1)}, u32[]{:S(2)}, u32[]{:S(2)}) collective-permute-start(f32[256,256]{1,0:T(8,128)S(1)} %get-tuple-element.78), channel_id=1, source_target_pairs={{0,1},{1,2},{2,3},{3,4},{4,5},{5,6},{6,7},{7,8},{8,9},{9,10},{10,1... | collective-permute-start | bytes 786440 | tf_op jit(solution)/shard_map/ppermute | solution.py:200
  53.6 14.8 %collective-permute-start.10 = (f32[256,256]{1,0:T(8,128)S(1)}, f32[256,256]{1,0:T(8,128)S(1)}, u32[]{:S(2)}, u32[]{:S(2)}) collective-permute-start(f32[256,256]{1,0:T(8,128)S(1)} %get-tuple-element.76), channel_id=1, source_target_pairs={{0,1},{1,2},{2,3},{3,4},{4,5},{5,6},{6,7},{7,8},{8,9},{9,10},{10,1... | collective-permute-start | bytes 786440 | tf_op jit(solution)/shard_map/ppermute | solution.py:200
where the time goes:
time: 69.7 us; the launch traced here: 69.5 us
  Pallas kernels  31.5 us (45%)
  waiting for transfers between devices  30.9 us (44%)
  starting transfers between devices  6.33 us (9%)
  between operations  0.8 us (1%)
    pallas_call x18, Pallas kernels, call(): pl.pallas_call(kernel, in_specs=[pl.BlockSpec(memory_space=s) for s in sp...  31.5 us
    ppermute x12, waiting for transfers between devices, move(): return lax.ppermute(block, ('outer', 'inner'), route)  30.9 us
    ppermute x12, starting transfers between devices, move(): return lax.ppermute(block, ('outer', 'inner'), route)  6.33 us
  transfers between devices with their start and end apart: 12, of which 10 were waited for; matrix products, arithmetic and copies ran while one was open for 0% of the time, Pallas kernels for 34%

commit v1 on v0

--- a/solution.py
+++ b/solution.py
@@ -19,6 +19,18 @@
     return lax.dot_general(
         a, b, (((ca,), (cb,)), ((), ())), precision=lax.Precision.HIGH, preferred_element_type=f32
     )
+
+
+def split(a):
+    high = a.astype(jnp.bfloat16)
+    return high, (a - high.astype(f32)).astype(jnp.bfloat16)
+
+
+def split_dot(a, b, ca, cb):
+    def product(p, q):
+        return lax.dot_general(p, q, (((ca,), (cb,)), ((), ())), preferred_element_type=f32)
+
+    return product(a[0], b[0]) + (product(a[0], b[1]) + product(a[1], b[0]))
 
 
 def adagrad(value, total, grad):
@@ -106,12 +118,13 @@
 def col_gradient(halves, t_ref, c_ref, M_refs, W_ref):
     n = M_refs[0].shape[1]
     cols = pl.ds(halves[0] * n, len(halves) * n)
-    C = jnp.concatenate([ref[:n, :] for ref in M_refs], axis=0)
+    C = split(jnp.concatenate([ref[:n, :] for ref in M_refs], axis=0))
     col_logs = jnp.concatenate([ref[n : n + 1, :] for ref in M_refs], axis=1)
     grad = None
     for rows in row_spans(W_ref.shape[0], 256):
-        W = W_ref[rows, :]
-        part = dot(errors(dot(W, C, 1, 1), t_ref[rows, cols], c_ref[rows, cols], col_logs), W, 0, 0)
+        W = split(W_ref[rows, :])
+        e = errors(split_dot(W, C, 1, 1), t_ref[rows, cols], c_ref[rows, cols], col_logs)
+        part = split_dot(split(e), W, 0, 0)
         grad = part if grad is None else grad + part
     return grad
 
@@ -226,7 +239,7 @@
                     [V(wide, f32), V(wide, f32), DMA((2, 2))], 20,
                 )
                 break
-            size, halves = 512, tuple(range(HALVES))
+            size, halves = (512, (0, 1)) if step == steps // 2 else (256, (0,))
             W, A, *grads = call(
                 functools.partial(row_col_kernel, size, halves, lambda rows: None), operands, [V] * 7,
                 [wide, wide] + [half] * len(halves), [V] * (2 + len(halves)), [], 20,

time: 69.7 us -> 68.8 us (0.987)
  waiting for transfers between devices: 30.9 us -> 28.4 us
  Pallas kernels: 31.5 us -> 32.6 us
    ppermute x12, waiting for transfers between devices: 30.9 us -> 28.4 us  [move(): return lax.ppermute(block, ('outer', 'inner'), route)]
    pallas_call x18 -> x19, Pallas kernels: 31.5 us -> 32.6 us  [call(): pl.pallas_call(kernel, in_specs=[pl.BlockSpec(memory_space=s) for s in sp...]
  transfers between devices with their start and end apart: 12 -> 12, of which waited for: 10 -> 11; matrix products, arithmetic and copies ran while one was open for 0% -> 0% of each run, Pallas kernels for 34% -> 36%
where the time goes in v1:
time: 68.8 us; the launch traced here: 68.6 us
  Pallas kernels  32.6 us (47%)
  waiting for transfers between devices  28.4 us (41%)
  starting transfers between devices  6.82 us (10%)
  between operations  0.8 us (1%)
    pallas_call x19, Pallas kernels, call(): pl.pallas_call(kernel, in_specs=[pl.BlockSpec(memory_space=s) for s in sp...  32.6 us
    ppermute x12, waiting for transfers between devices, move(): return lax.ppermute(block, ('outer', 'inner'), route)  28.4 us
    ppermute x12, starting transfers between devices, move(): return lax.ppermute(block, ('outer', 'inner'), route)  6.82 us
  transfers between devices with their start and end apart: 12, of which 11 were waited for; matrix products, arithmetic and copies ran while one was open for 0% of the time, Pallas kernels for 36%

profile of v1, /device:TPU:0, one launch (start us, length us, event | category | flops | bytes accessed | tf_op | source)
XLA Modules:
  0.0 68.6 jit_solution(10773613050220128382)
XLA Ops:
  0.6 6.4 %shard_map.102 = (f32[1024,256]{1,0:T(8,128)S(1)}, f32[1024,256]{1,0:T(8,128)S(1)}, f32[1024,512]{1,0:T(8,128)S(1)}, f32[1024,512]{1,0:T(8,128)S(1)}, f32[256,25...) custom-call(s32[1,4,1024,512]{3,2,1,0:T(8,128)} %x_hbm.7, ...), custom_call_target="tpu_custom_call" | custom-call | tf_op jit(solution)/shard_map/pallas_call | solution.py:193
  7.3 1.6 %shard_map.104.h_ref = f32[256,256]{1,0:T(8,128)S(1)} custom-call(f32[1024,512]{1,0:T(8,128)S(1)} %get-tuple-element.51.t_ref, f32[1024,512]{1,0:T(8,128)S(1)} %get-tuple-element.52.c_ref, f32[264,256]{1,0:T(8,128)S(1)} %get-tuple-element.53.M_ref, f32[1024,256]{1,0:T(8,128)S(1)} %get-tuple-element.54.W_ref), custom_call_target="tpu_custom_call" | custom-call | tf_op jit(solution)/shard_map/pallas_call | solution.py:193
  8.9 1.8 %collective-permute-start.1 = (f32[264,256]{1,0:T(8,128)S(1)}, f32[264,256]{1,0:T(8,128)S(1)}, u32[]{:S(2)}, u32[]{:S(2)}) collective-permute-start(f32[264,256]{1,0:T(8,128)S(1)} %get-tuple-element.61), channel_id=1, source_target_pairs={{0,1},{1,2},{2,3},{3,4},{4,5},{5,6},{6,7},{7,8},{8,9},{9,10},{10,1... | collective-permute-start | bytes 811016 | tf_op jit(solution)/shard_map/ppermute | solution.py:213
  10.9 1.4 %collective-permute-start.3 = (f32[256,256]{1,0:T(8,128)S(1)}, f32[256,256]{1,0:T(8,128)S(1)}, u32[]{:S(2)}, u32[]{:S(2)}) collective-permute-start(f32[256,256]{1,0:T(8,128)S(1)} %get-tuple-element.56), channel_id=1, source_target_pairs={{0,1},{1,2},{2,3},{3,4},{4,5},{5,6},{6,7},{7,8},{8,9},{9,10},{10,1... | collective-permute-start | bytes 786440 | tf_op jit(solution)/shard_map/ppermute | solution.py:213
  12.3 1.9 %shard_map.106 = (f32[1024,512]{1,0:T(8,128)S(1)}, f32[1024,512]{1,0:T(8,128)S(1)}) custom-call(s32[1,4,1024,512]{3,2,1,0:T(8,128)} %x_hbm.7, s32[8,128]{1,0:T(8,128)S(1)} %bitcast.3), custom_call_target="tpu_custom_call" | custom-call | tf_op jit(solution)/shard_map/pallas_call | solution.py:193
  14.2 4.0 %collective-permute-done.M_ref.M0_ref = f32[264,256]{1,0:T(8,128)S(1)} collective-permute-done((f32[264,256]{1,0:T(8,128)S(1)}, f32[264,256]{1,0:T(8,128)S(1)}, u32[]{:S(2)}, u32[]{:S(2)}) %collective-permute-start) | collective-permute-done | bytes 270368 | tf_op jit(solution)/shard_map/ppermute | solution.py:213
  18.2 1.6 %shard_map.107.g_ref = f32[1024,256]{1,0:T(8,128)S(1)} custom-call(f32[1024,512]{1,0:T(8,128)S(1)} %get-tuple-element.58.t_ref, f32[1024,512]{1,0:T(8,128)S(1)} %get-tuple-element.59.c_ref, f32[264,256]{1,0:T(8,128)S(1)} %collective-permute-done.M_ref.M0_ref, f32[1024,256]{1,0:T(8,128)S(1)} %get-tuple-element.54.W_ref), custom_call_target="tpu_custom_call" | custom-call | tf_op jit(solution)/shard_map/pallas_call | solution.py:193
  19.7 1.3 %collective-permute-done.1.M1_ref.M_ref = f32[264,256]{1,0:T(8,128)S(1)} collective-permute-done((f32[264,256]{1,0:T(8,128)S(1)}, f32[264,256]{1,0:T(8,128)S(1)}, u32[]{:S(2)}, u32[]{:S(2)}) %collective-permute-start.1) | collective-permute-done | bytes 270368 | tf_op jit(solution)/shard_map/ppermute | solution.py:213
  21.1 2.7 %shard_map.108 = (f32[1024,256]{1,0:T(8,128)S(1)}, f32[1024,256]{1,0:T(8,128)S(1)}, f32[256,256]{1,0:T(8,128)S(1)}) custom-call(f32[1024,512]{1,0:T(8,128)S(1)} %get-tuple-element.58.t_ref, f32[1024,512]{1,0:T(8,128)S(1)} %get-tuple-element.59.c_ref, f32[264,256]{1,0:T(8,128)S(1)} %collective-permute-done.M_ref.M0_ref, ...), custom_call_target="tpu_custom_call" | custom-call | tf_op jit(solution)/shard_map/pallas_call | solution.py:193
  24.0 1.6 %shard_map.110.h_ref = f32[256,256]{1,0:T(8,128)S(1)} custom-call(f32[1024,512]{1,0:T(8,128)S(1)} %get-tuple-element.58.t_ref, f32[1024,512]{1,0:T(8,128)S(1)} %get-tuple-element.59.c_ref, f32[264,256]{1,0:T(8,128)S(1)} %collective-permute-done.1.M1_ref.M_ref, f32[1024,256]{1,0:T(8,128)S(1)} %get-tuple-element.65.W_ref), custom_call_target="tpu_custom_call" | custom-call | tf_op jit(solution)/shard_map/pallas_call | solution.py:193
  26.9 1.3 %collective-permute-start.7 = (f32[256,256]{1,0:T(8,128)S(1)}, f32[256,256]{1,0:T(8,128)S(1)}, u32[]{:S(2)}, u32[]{:S(2)}) collective-permute-start(f32[256,256]{1,0:T(8,128)S(1)} %get-tuple-element.66), channel_id=1, source_target_pairs={{0,65},{1,66},{2,67},{3,68},{4,69},{5,70},{6,71},{7,72},{8,73},{9,... | collective-permute-start | bytes 786440 | tf_op jit(solution)/shard_map/ppermute | solution.py:213
  28.3 1.9 %shard_map.112 = (f32[1024,512]{1,0:T(8,128)S(1)}, f32[1024,512]{1,0:T(8,128)S(1)}) custom-call(s32[1,4,1024,512]{3,2,1,0:T(8,128)} %x_hbm.7, s32[8,128]{1,0:T(8,128)S(1)} %bitcast.4), custom_call_target="tpu_custom_call" | custom-call | tf_op jit(solution)/shard_map/pallas_call | solution.py:193
  30.2 7.3 %collective-permute-done.4.M_ref.M0_ref = f32[264,256]{1,0:T(8,128)S(1)} collective-permute-done((f32[264,256]{1,0:T(8,128)S(1)}, f32[264,256]{1,0:T(8,128)S(1)}, u32[]{:S(2)}, u32[]{:S(2)}) %collective-permute-start.4) | collective-permute-done | bytes 270368 | tf_op jit(solution)/shard_map/ppermute | solution.py:213
  37.5 1.6 %shard_map.113.g_ref = f32[1024,256]{1,0:T(8,128)S(1)} custom-call(f32[1024,512]{1,0:T(8,128)S(1)} %get-tuple-element.68.t_ref, f32[1024,512]{1,0:T(8,128)S(1)} %get-tuple-element.69.c_ref, f32[264,256]{1,0:T(8,128)S(1)} %collective-permute-done.4.M_ref.M0_ref, f32[1024,256]{1,0:T(8,128)S(1)} %get-tuple-element.65.W_ref), custom_call_target="tpu_custom_call" | custom-call | tf_op jit(solution)/shard_map/pallas_call | solution.py:193
  39.1 3.2 %collective-permute-done.5.M1_ref.M_ref = f32[264,256]{1,0:T(8,128)S(1)} collective-permute-done((f32[264,256]{1,0:T(8,128)S(1)}, f32[264,256]{1,0:T(8,128)S(1)}, u32[]{:S(2)}, u32[]{:S(2)}) %collective-permute-start.5) | collective-permute-done | bytes 270368 | tf_op jit(solution)/shard_map/ppermute | solution.py:213
  42.3 3.9 %shard_map.114 = (f32[1024,256]{1,0:T(8,128)S(1)}, f32[1024,256]{1,0:T(8,128)S(1)}, f32[256,256]{1,0:T(8,128)S(1)}, f32[256,256]{1,0:T(8,128)S(1)}) custom-call(f32[1024,512]{1,0:T(8,128)S(1)} %get-tuple-element.68.t_ref, f32[1024,512]{1,0:T(8,128)S(1)} %get-tuple-element.69.c_ref, f32[264,256]{1,0:T(8,128)S(1)} %collective-permute-done.4.M_ref.M0_ref, ...), custom_call_target="tpu_custom_call" | custom-call | tf_op jit(solution)/shard_map/pallas_call | solution.py:193
  47.7 3.9 %collective-permute-done.7.B_ref = f32[256,256]{1,0:T(8,128)S(1)} collective-permute-done((f32[256,256]{1,0:T(8,128)S(1)}, f32[256,256]{1,0:T(8,128)S(1)}, u32[]{:S(2)}, u32[]{:S(2)}) %collective-permute-start.7) | collective-permute-done | bytes 262176 | tf_op jit(solution)/shard_map/ppermute | solution.py:213
  52.9 1.9 %shard_map.117 = (f32[1024,512]{1,0:T(8,128)S(1)}, f32[1024,512]{1,0:T(8,128)S(1)}) custom-call(s32[1,4,1024,512]{3,2,1,0:T(8,128)} %x_hbm.7, s32[8,128]{1,0:T(8,128)S(1)} %bitcast.5), custom_call_target="tpu_custom_call" | custom-call | tf_op jit(solution)/shard_map/pallas_call | solution.py:193
  54.8 2.4 %collective-permute-done.8.M_ref.refs_2_.refs_1_ = f32[264,256]{1,0:T(8,128)S(1)} collective-permute-done((f32[264,256]{1,0:T(8,128)S(1)}, f32[264,256]{1,0:T(8,128)S(1)}, u32[]{:S(2)}, u32[]{:S(2)}) %collective-permute-start.8) | collective-permute-done | bytes 270368 | tf_op jit(solution)/shard_map/ppermute | solution.py:213
  57.2 1.6 %shard_map.118.refs_6_ = f32[1024,256]{1,0:T(8,128)S(1)} custom-call(f32[1024,512]{1,0:T(8,128)S(1)} %get-tuple-element.78.t_ref.refs_0_, f32[1024,512]{1,0:T(8,128)S(1)} %get-tuple-element.79.c_ref.refs_1_, f32[264,256]{1,0:T(8,128)S(1)} %collective-permute-done.8.M_ref.refs_2_.refs_1_, f32[1024,256]{1,0:T(8,128)S(1)} %get-tuple-element.82.W_ref.refs_4_), custom_call_target="tpu_custom_call" | custom-call | tf_op jit(solution)/shard_map/pallas_call | solution.py:193
  58.8 3.1 %collective-permute-done.9.refs_3_.refs_4_ = f32[264,256]{1,0:T(8,128)S(1)} collective-permute-done((f32[264,256]{1,0:T(8,128)S(1)}, f32[264,256]{1,0:T(8,128)S(1)}, u32[]{:S(2)}, u32[]{:S(2)}) %collective-permute-start.9) | collective-permute-done | bytes 270368 | tf_op jit(solution)/shard_map/ppermute | solution.py:213
  61.9 4.4 %shard_map.119 = (f32[1024,256]{1,0:T(8,128)}, f32[1024,256]{1,0:T(8,128)}, f32[256,256]{1,0:T(8,128)S(1)}, f32[256,256]{1,0:T(8,128)S(1)}) custom-call(f32[1024,512]{1,0:T(8,128)S(1)} %get-tuple-element.78.t_ref.refs_0_, f32[1024,512]{1,0:T(8,128)S(1)} %get-tuple-element.79.c_ref.refs_1_, f32[264,256]{1,0:T(8,128)S(1)} %collective-permute-done.8.M_ref.refs_2_.refs_1_, ...), custom_call_target="tpu_custom_call" | custom-call | tf_op jit(solution)/shard_map/pallas_call | solution.py:193
  66.3 1.2 %collective-permute-done.10.refs_2_ = f32[256,256]{1,0:T(8,128)S(1)} collective-permute-done((f32[256,256]{1,0:T(8,128)S(1)}, f32[256,256]{1,0:T(8,128)S(1)}, u32[]{:S(2)}, u32[]{:S(2)}) %collective-permute-start.10) | collective-permute-done | bytes 262176 | tf_op jit(solution)/shard_map/ppermute | solution.py:213
  67.5 1.1 %shard_map.120 = (f32[512,256]{1,0:T(8,128)}, f32[512,256]{1,0:T(8,128)}) custom-call(f32[256,256]{1,0:T(8,128)S(1)} %get-tuple-element.86.refs_0_, f32[264,256]{1,0:T(8,128)S(1)} %collective-permute-done.8.M_ref.refs_2_.refs_1_, f32[256,256]{1,0:T(8,128)S(1)} %collective-permute-done.10.refs_2_, f32[256,256]{1,0:T(8,128)S(1)} %get-tuple-element.87.refs_3_, ...), custom_call_target="tpu_custom_call" | custom-call | tf_op jit(solution)/shard_map/pallas_call | solution.py:193
  (21 shorter events, 4.6 us)
Async XLA Ops:
  7.2 11.0 %collective-permute-start = (f32[264,256]{1,0:T(8,128)S(1)}, f32[264,256]{1,0:T(8,128)S(1)}, u32[]{:S(2)}, u32[]{:S(2)}) collective-permute-start(f32[264,256]{1,0:T(8,128)S(1)} %get-tuple-element.60), channel_id=1, source_target_pairs={{0,1},{1,2},{2,3},{3,4},{4,5},{5,6},{6,7},{7,8},{8,9},{9,10},{10,1... | collective-permute-start | bytes 811016 | tf_op jit(solution)/shard_map/ppermute | solution.py:213
  7.2 5.0 %copy-start = (s32[1024]{0:T(1024)S(1)}, s32[1024]{0:T(1024)}, u32[]{:S(2)}) copy-start(s32[1024]{0:T(1024)} %param.8) | copy-start | bytes 12292
  8.9 12.1 %collective-permute-start.1 = (f32[264,256]{1,0:T(8,128)S(1)}, f32[264,256]{1,0:T(8,128)S(1)}, u32[]{:S(2)}, u32[]{:S(2)}) collective-permute-start(f32[264,256]{1,0:T(8,128)S(1)} %get-tuple-element.61), channel_id=1, source_target_pairs={{0,1},{1,2},{2,3},{3,4},{4,5},{5,6},{6,7},{7,8},{8,9},{9,10},{10,1... | collective-permute-start | bytes 811016 | tf_op jit(solution)/shard_map/ppermute | solution.py:213
  10.8 13.1 %collective-permute-start.2 = (f32[256,256]{1,0:T(8,128)S(1)}, f32[256,256]{1,0:T(8,128)S(1)}, u32[]{:S(2)}, u32[]{:S(2)}) collective-permute-start(f32[256,256]{1,0:T(8,128)S(1)} %get-tuple-element.50), channel_id=1, source_target_pairs={{0,1},{1,2},{2,3},{3,4},{4,5},{5,6},{6,7},{7,8},{8,9},{9,10},{10,1... | collective-permute-start | bytes 786440 | tf_op jit(solution)/shard_map/ppermute | solution.py:213
  10.9 15.8 %collective-permute-start.3 = (f32[256,256]{1,0:T(8,128)S(1)}, f32[256,256]{1,0:T(8,128)S(1)}, u32[]{:S(2)}, u32[]{:S(2)}) collective-permute-start(f32[256,256]{1,0:T(8,128)S(1)} %get-tuple-element.56), channel_id=1, source_target_pairs={{0,1},{1,2},{2,3},{3,4},{4,5},{5,6},{6,7},{7,8},{8,9},{9,10},{10,1... | collective-permute-start | bytes 786440 | tf_op jit(solution)/shard_map/ppermute | solution.py:213
  23.9 13.6 %collective-permute-start.4 = (f32[264,256]{1,0:T(8,128)S(1)}, f32[264,256]{1,0:T(8,128)S(1)}, u32[]{:S(2)}, u32[]{:S(2)}) collective-permute-start(f32[264,256]{1,0:T(8,128)S(1)} %get-tuple-element.70), channel_id=1, source_target_pairs={{0,65},{1,66},{2,67},{3,68},{4,69},{5,70},{6,71},{7,72},{8,73},{9,... | collective-permute-start | bytes 811016 | tf_op jit(solution)/shard_map/ppermute | solution.py:213
  26.8 15.5 %collective-permute-start.5 = (f32[264,256]{1,0:T(8,128)S(1)}, f32[264,256]{1,0:T(8,128)S(1)}, u32[]{:S(2)}, u32[]{:S(2)}) collective-permute-start(f32[264,256]{1,0:T(8,128)S(1)} %get-tuple-element.71), channel_id=1, source_target_pairs={{0,65},{1,66},{2,67},{3,68},{4,69},{5,70},{6,71},{7,72},{8,73},{9,... | collective-permute-start | bytes 811016 | tf_op jit(solution)/shard_map/ppermute | solution.py:213
  26.8 20.1 %collective-permute-start.6 = (f32[256,256]{1,0:T(8,128)S(1)}, f32[256,256]{1,0:T(8,128)S(1)}, u32[]{:S(2)}, u32[]{:S(2)}) collective-permute-start(f32[256,256]{1,0:T(8,128)S(1)} %get-tuple-element.64), channel_id=1, source_target_pairs={{0,65},{1,66},{2,67},{3,68},{4,69},{5,70},{6,71},{7,72},{8,73},{9,... | collective-permute-start | bytes 786440 | tf_op jit(solution)/shard_map/ppermute | solution.py:213
  26.9 24.7 %collective-permute-start.7 = (f32[256,256]{1,0:T(8,128)S(1)}, f32[256,256]{1,0:T(8,128)S(1)}, u32[]{:S(2)}, u32[]{:S(2)}) collective-permute-start(f32[256,256]{1,0:T(8,128)S(1)} %get-tuple-element.66), channel_id=1, source_target_pairs={{0,65},{1,66},{2,67},{3,68},{4,69},{5,70},{6,71},{7,72},{8,73},{9,... | collective-permute-start | bytes 786440 | tf_op jit(solution)/shard_map/ppermute | solution.py:213
  47.0 10.2 %collective-permute-start.8 = (f32[264,256]{1,0:T(8,128)S(1)}, f32[264,256]{1,0:T(8,128)S(1)}, u32[]{:S(2)}, u32[]{:S(2)}) collective-permute-start(f32[264,256]{1,0:T(8,128)S(1)} %get-tuple-element.80), channel_id=1, source_target_pairs={{0,1},{1,2},{2,3},{3,4},{4,5},{5,6},{6,7},{7,8},{8,9},{9,10},{10,1... | collective-permute-start | bytes 811016 | tf_op jit(solution)/shard_map/ppermute | solution.py:213
  51.7 10.2 %collective-permute-start.9 = (f32[264,256]{1,0:T(8,128)S(1)}, f32[264,256]{1,0:T(8,128)S(1)}, u32[]{:S(2)}, u32[]{:S(2)}) collective-permute-start(f32[264,256]{1,0:T(8,128)S(1)} %get-tuple-element.81), channel_id=1, source_target_pairs={{0,1},{1,2},{2,3},{3,4},{4,5},{5,6},{6,7},{7,8},{8,9},{9,10},{10,1... | collective-permute-start | bytes 811016 | tf_op jit(solution)/shard_map/ppermute | solution.py:213
  52.4 13.9 %collective-permute-start.11 = (f32[256,256]{1,0:T(8,128)S(1)}, f32[256,256]{1,0:T(8,128)S(1)}, u32[]{:S(2)}, u32[]{:S(2)}) collective-permute-start(f32[256,256]{1,0:T(8,128)S(1)} %get-tuple-element.76), channel_id=1, source_target_pairs={{0,1},{1,2},{2,3},{3,4},{4,5},{5,6},{6,7},{7,8},{8,9},{9,10},{10,1... | collective-permute-start | bytes 786440 | tf_op jit(solution)/shard_map/ppermute | solution.py:213
  52.5 15.0 %collective-permute-start.10 = (f32[256,256]{1,0:T(8,128)S(1)}, f32[256,256]{1,0:T(8,128)S(1)}, u32[]{:S(2)}, u32[]{:S(2)}) collective-permute-start(f32[256,256]{1,0:T(8,128)S(1)} %get-tuple-element.74), channel_id=1, source_target_pairs={{0,1},{1,2},{2,3},{3,4},{4,5},{5,6},{6,7},{7,8},{8,9},{9,10},{10,1... | collective-permute-start | bytes 786440 | tf_op jit(solution)/shard_map/ppermute | solution.py:213
